TPU v7x, 512 devices: a whole 4x8x8 slice. The times are simulated.
512 devices in a mesh: group: 64 (over x, z_lo, y), shard: 8 (over z_hi, core).
Axes of the slice: x: 4, y: 8, z: 8 (z_hi: 4, z_lo: 2; z = z_hi * 2 + z_lo), core: 2. Of those that a mesh axis runs over, the one named last changes fastest.
Arguments:
- owners: int32 [6], replicated, may hold values from 0 to 7, as said below
- mat_weight: bfloat16 [6, 128, 4096], P(None, 'shard'), may hold values from -0.09375 to 0.09375
- mat_grad: bfloat16 [64, 6, 128, 4096], P('group', None, 'shard'), may hold values from -2 to 2
- head_block_momentum: bfloat16 [6, 128, 4096], P(None, 'shard'), may hold values from -48 to 48
- emb_weight: bfloat16 [256, 4096], P('shard'), may hold values from -6 to 6
- emb_grad: bfloat16 [64, 256, 4096], P('group', 'shard'), may hold values from -2 to 2
- emb_first: float32 [256, 4096], P('shard'), may hold values from -6 to 6
- emb_second: float32 [256, 4096], P('shard'), may hold values from 0.1 to 10
- norm_weight: bfloat16 [2, 4096], P(None, 'shard'), may hold values from 0.5 to 1.5
- norm_grad: bfloat16 [64, 2, 4096], P('group', None, 'shard'), may hold values from -2 to 2
- norm_first: float32 [2, 4096], P(None, 'shard'), may hold values from -6 to 6
- norm_second: float32 [2, 4096], P(None, 'shard'), may hold values from 0.1 to 10
- qk_weight: bfloat16 [2, 128], replicated, may hold values from 0.5 to 1.5
- qk_grad: bfloat16 [64, 2, 128], P('group'), may hold values from -2 to 2
- qk_first: float32 [2, 128], replicated, may hold values from -6 to 6
- qk_second: float32 [2, 128], replicated, may hold values from 0.1 to 10
Outputs:
- new_weight: bfloat16 [6, 128, 4096], P(None, 'shard')
- new_moment: bfloat16 [6, 128, 4096], P(None, 'shard')
- owner_sums: float32 [8, 1], P('shard')
- emb_new: bfloat16 [256, 4096], P('shard')
- emb_first_new: float32 [256, 4096], P('shard')
- emb_second_new: float32 [256, 4096], P('shard')
- norm_new: bfloat16 [2, 4096], P(None, 'shard')
- norm_first_new: float32 [2, 4096], P(None, 'shard')
- norm_second_new: float32 [2, 4096], P(None, 'shard')
- qk_new: bfloat16 [2, 128], replicated
- qk_first_new: float32 [2, 128], replicated
- qk_second_new: float32 [2, 128], replicated
Inputs may be any that keep to these rules, and one draw needn't show every extreme that they name: `owners`: each shard rank owns at most 1 head blocks, and some rank owns exactly 1.
All inputs are finite; a program needn't handle non-finite values.
Results may differ from a plain program's by a relative error of at most 0.008.
Values may be sent and summed in bfloat16 or wider, within the bound.
No kernel may reach another device: no remote copies, remote signals or barrier semaphores. Data moves between devices by JAX's collectives and lax.ppermute only.
A program may use at most 64 MiB of HBM per device.

v0:
```python
import math

import jax
import jax.numpy as jnp
from jax import lax
from jax.sharding import PartitionSpec as P

D = 4096
HEAD = 128
MATS = 6
NS_ITERS = 5


momentum_decay = 0.95
muon_rate = 0.02
weight_decay = 0.1
adam_rate = 0.01
beta_first = 0.9
beta_second = 0.95
adam_epsilon = 1e-08
bias_first = 1.0 - 0.9**10
bias_second = 1.0 - 0.95**10
norm_epsilon = 1e-07
quintic_a = 3.4445
quintic_b = -4.775
quintic_c = 2.0315


def orthogonalize(matrix):
    widened = matrix.astype(jnp.float32)
    iterate = (widened / (jnp.sqrt(jnp.sum(widened * widened)) + norm_epsilon)).astype(jnp.bfloat16)
    for sweep in range(NS_ITERS):
        gram = jnp.dot(iterate, iterate.T, preferred_element_type=jnp.float32).astype(jnp.bfloat16)
        squared = jnp.dot(gram, gram, preferred_element_type=jnp.float32)
        blend = (quintic_b * gram.astype(jnp.float32) + quintic_c * squared).astype(jnp.bfloat16)
        iterate = (
            quintic_a * iterate.astype(jnp.float32)
            + jnp.dot(blend, iterate, preferred_element_type=jnp.float32)
        ).astype(jnp.bfloat16)
    return iterate


def slot_energy(ortho, pushed):
    return jnp.sum(ortho.astype(jnp.float32) * pushed.astype(jnp.float32), axis=(1, 2)) / (
        HEAD * math.sqrt(D)
    )


def owner_slots(owners, capacity):
    order = jnp.arange(owners.shape[0], dtype=jnp.int32)
    same = (owners[:, None] == owners[None, :]) & (order[None, :] < order[:, None])
    position = jnp.sum(same.astype(jnp.int32), axis=1)
    return owners * capacity + position


def adamw(weight, grad_sum, first, second):
    first_new = beta_first * first + (1.0 - beta_first) * grad_sum
    second_new = beta_second * second + (1.0 - beta_second) * grad_sum * grad_sum
    wide_weight = weight.astype(jnp.float32)
    stepped = (
        first_new / bias_first / (jnp.sqrt(second_new / bias_second) + adam_epsilon)
        + weight_decay * wide_weight
    )
    return ((wide_weight - adam_rate * stepped).astype(jnp.bfloat16), first_new, second_new)


def on_device(
    owners,
    mat_weight,
    mat_grad,
    head_block_momentum,
    emb_weight,
    emb_grad,
    emb_first,
    emb_second,
    norm_weight,
    norm_grad,
    norm_first,
    norm_second,
    qk_weight,
    qk_grad,
    qk_first,
    qk_second,
):
    shards = lax.axis_size("shard")
    capacity = -(-MATS // shards)
    rows = mat_weight.shape[1]
    width = mat_weight.shape[2]
    muon_scale = 0.2 * math.sqrt(max(HEAD, D))
    local_grad = mat_grad[0].astype(jnp.float32)
    grad_total, emb_total, norm_total, qk_total = lax.psum(
        (
            local_grad,
            emb_grad[0].astype(jnp.float32),
            norm_grad[0].astype(jnp.float32),
            qk_grad[0].astype(jnp.float32),
        ),
        "group",
    )
    moment_wide = momentum_decay * head_block_momentum.astype(jnp.float32) + grad_total
    new_moment = moment_wide.astype(jnp.bfloat16)
    forwarded_rows = (grad_total + momentum_decay * moment_wide).astype(jnp.bfloat16)
    slots = owner_slots(owners, capacity)
    places = jnp.arange(shards * capacity, dtype=jnp.int32)
    gather_rows_back = (slots[:, None] == places[None, :]).astype(jnp.bfloat16)
    outgoing = jnp.einsum(
        "of,oyq->fyq", gather_rows_back, forwarded_rows, preferred_element_type=jnp.float32
    ).astype(jnp.bfloat16)
    outgoing = outgoing.reshape(shards, capacity, rows, width)
    items = lax.all_to_all(outgoing, "shard", split_axis=0, concat_axis=2, tiled=True)
    ortho = lax.map(orthogonalize, items[0])
    returned = lax.all_to_all(ortho[None], "shard", split_axis=2, concat_axis=0, tiled=True)
    returned, owner_sums = (returned, slot_energy(ortho, items[0])[None])
    kept_row_block = returned.reshape(shards * capacity, rows, width)
    muon_update = jnp.einsum(
        "ar,rpx->apx", gather_rows_back, kept_row_block, preferred_element_type=jnp.float32
    )
    new_weight = (
        mat_weight.astype(jnp.float32) * (1.0 - muon_rate * weight_decay)
        - muon_rate * muon_scale * muon_update
    ).astype(jnp.bfloat16)
    emb_new, emb_first_new, emb_second_new = adamw(emb_weight, emb_total, emb_first, emb_second)
    norm_new, norm_first_new, norm_second_new = adamw(
        norm_weight, norm_total, norm_first, norm_second
    )
    qk_new, qk_first_new, qk_second_new = adamw(qk_weight, qk_total, qk_first, qk_second)
    return (
        new_weight,
        new_moment,
        owner_sums,
        emb_new,
        emb_first_new,
        emb_second_new,
        norm_new,
        norm_first_new,
        norm_second_new,
        qk_new,
        qk_first_new,
        qk_second_new,
    )


def solution(mesh):
    placed = (
        P(),
        P(None, "shard", None),
        P("group", None, "shard", None),
        P(None, "shard", None),
        P("shard", None),
        P("group", "shard", None),
        P("shard", None),
        P("shard", None),
        P(None, "shard"),
        P("group", None, "shard"),
        P(None, "shard"),
        P(None, "shard"),
        P(),
        P("group", None, None),
        P(),
        P(),
    )
    return jax.shard_map(
        on_device,
        mesh=mesh,
        in_specs=placed,
        out_specs=(
            P(None, "shard", None),
            P(None, "shard", None),
            P("shard", None),
            P("shard", None),
            P("shard", None),
            P("shard", None),
            P(None, "shard"),
            P(None, "shard"),
            P(None, "shard"),
            P(),
            P(),
            P(),
        ),
        check_vma=False,
    )
```

profile of v0, /device:TPU:128, one launch (start us, length us, event | category | flops | bytes accessed | tf_op | source)
XLA Modules:
  0.0 869.8 jit_solution(506316435422333019)
XLA Ops:
  7.3 2.5 bitcast_convert_fusion
  9.8 0.8 bitcast_convert_fusion.1
  10.8 622.3 %all-reduce.4.cloned.1.call-done = (f32[6,16,4096]{2,1,0:T(8,128)}, f32[32,4096]{1,0:T(8,128)}) async-done(((f32[6,16,4096]{2,1,0:T(8,128)}, f32[32,4096]{1,0:T(8,128)}), (f32[6,16,4096]{2,1,0:T(8,128)}, f32[32,4096]{1,0:T(8,128)})) %all-reduce.4.cloned.1.call-update) | async-done | bytes 2097168 | tf_op jit(solution)/shard_map/psum | solution.py:91
  633.1 2.6 fusion.12
  635.7 1.1 fusion.7
  636.8 0.6 copy.58
  637.4 27.0 %all_to_all.8 = bf16[8,1,16,4096]{3,2,1,0:T(8,128)(2,1)S(1)} all-to-all(bf16[8,1,16,4096]{3,2,1,0:T(8,128)(2,1)S(1)} %copy.58), channel_id=1, replica_groups=mesh['group'=64,'shard'=8] {'shard'}, dimensions={0} | all-to-all | bytes 2097152 | tf_op jit(solution)/shard_map/all_to_all | solution.py:110
  664.5 1.1 fusion.8
  666.5 0.4 convolution_convert_fusion.5
  666.9 0.2 fusion.10
  667.1 0.6 fusion.1
  667.7 0.4 convolution_convert_fusion.4
  668.1 0.6 fusion.2
  668.7 0.4 convolution_convert_fusion.3
  669.1 0.6 fusion.3
  669.7 0.4 convolution_convert_fusion.2
  670.1 0.6 fusion.4
  670.7 0.4 convolution_convert_fusion.1
  671.1 2.3 fusion.11
  673.4 3.6 copy.72
  677.0 0.5 broadcast.107
  677.5 7.2 reduce.4
  684.9 1.6 reshape.83
  686.5 7.1 all-to-all-start.1
  693.6 159.3 %all-reduce = (f32[2,512]{1,0:T(2,128)S(1)}, f32[2,128]{1,0:T(2,128)S(1)}) all-reduce(f32[2,512]{1,0:T(2,128)S(1)} %bitcast_convert_fusion.2, f32[2,128]{1,0:T(2,128)S(1)} %bitcast_convert_fusion.3), channel_id=1, replica_groups=mesh['group'=64,'shard'=8] {'group'}, use_global_device_ids=true, to_apply=%region_5.6 | all-reduce | flops 1280 | bytes 10240 | tf_op jit(solution)/shard_map/psum | solution.py:91
  852.9 0.6 fusion.62
  853.5 0.6 fusion.56
  854.1 1.3 fusion.27
  856.1 1.1 reshape.84
  857.2 1.1 copy.65
  858.3 2.2 fusion.6
  860.5 1.3 copy.62
  (40 shorter events, 0.5 us)
Async XLA Ops:
  7.2 2.6 copy-start.4
  7.2 3.4 copy-start.14
  7.2 625.9 %copy-start = (bf16[6,16,4096]{2,1,0:T(8,128)(2,1)S(1)}, bf16[6,16,4096]{2,1,0:T(8,128)(2,1)}, u32[]{:S(2)}) copy-start(bf16[6,16,4096]{2,1,0:T(8,128)(2,1)} %param.19) | copy-start | bytes 2359300
  7.2 625.9 %all-reduce.4.cloned.1.call-start = ((), (), s32[]{:S(2)}) async-start(), calls=%async_computation.2 | async-start | bytes 4194304 | tf_op jit(solution)/shard_map/psum | solution.py:91
  684.8 8.8 %copy-start.15 = (bf16[1,2,128]{2,1,0:T(2,128)(2,1)S(1)}, bf16[1,2,128]{2,1,0:T(2,128)(2,1)}, u32[]{:S(2)}) copy-start(bf16[1,2,128]{2,1,0:T(2,128)(2,1)} %param.29) | copy-start | bytes 1540
  684.8 8.8 %copy-start.8 = (bf16[1,2,512]{2,1,0:T(2,128)(2,1)S(1)}, bf16[1,2,512]{2,1,0:T(2,128)(2,1)}, u32[]{:S(2)}) copy-start(bf16[1,2,512]{2,1,0:T(2,128)(2,1)} %param.25) | copy-start | bytes 6148
  684.8 168.1 %copy-start.10 = (f32[2,128]{1,0:T(2,128)S(1)}, f32[2,128]{1,0:T(2,128)}, u32[]{:S(2)}) copy-start(f32[2,128]{1,0:T(2,128)} %param.30) | copy-start | bytes 3076
  684.8 168.1 %copy-start.11 = (f32[2,128]{1,0:T(2,128)S(1)}, f32[2,128]{1,0:T(2,128)}, u32[]{:S(2)}) copy-start(f32[2,128]{1,0:T(2,128)} %param.31) | copy-start | bytes 3076
  684.8 168.1 %copy-start.12 = (bf16[2,128]{1,0:T(2,128)(2,1)S(1)}, bf16[2,128]{1,0:T(2,128)(2,1)}, u32[]{:S(2)}) copy-start(bf16[2,128]{1,0:T(2,128)(2,1)} %param.28) | copy-start | bytes 1540
  684.8 168.6 %copy-start.6 = (f32[2,512]{1,0:T(2,128)S(1)}, f32[2,512]{1,0:T(2,128)}, u32[]{:S(2)}) copy-start(f32[2,512]{1,0:T(2,128)} %param.26) | copy-start | bytes 12292
  684.8 168.6 %copy-start.7 = (f32[2,512]{1,0:T(2,128)S(1)}, f32[2,512]{1,0:T(2,128)}, u32[]{:S(2)}) copy-start(f32[2,512]{1,0:T(2,128)} %param.27) | copy-start | bytes 12292
  684.9 168.6 %copy-start.9 = (bf16[2,512]{1,0:T(2,128)(2,1)S(1)}, bf16[2,512]{1,0:T(2,128)(2,1)}, u32[]{:S(2)}) copy-start(bf16[2,512]{1,0:T(2,128)(2,1)} %param.24) | copy-start | bytes 6148
  684.9 169.2 %copy-start.1 = (f32[32,4096]{1,0:T(8,128)S(1)}, f32[32,4096]{1,0:T(8,128)}, u32[]{:S(2)}) copy-start(f32[32,4096]{1,0:T(8,128)} %param.22) | copy-start | bytes 1572868
  684.9 169.2 %copy-start.2 = (f32[32,4096]{1,0:T(8,128)S(1)}, f32[32,4096]{1,0:T(8,128)}, u32[]{:S(2)}) copy-start(f32[32,4096]{1,0:T(8,128)} %param.23) | copy-start | bytes 1572868
  684.9 169.2 %copy-start.5 = (bf16[32,4096]{1,0:T(8,128)(2,1)S(1)}, bf16[32,4096]{1,0:T(8,128)(2,1)}, u32[]{:S(2)}) copy-start(bf16[32,4096]{1,0:T(8,128)(2,1)} %param.20) | copy-start | bytes 786436
  686.5 167.6 %copy-start.3 = (f32[32,4096]{1,0:T(8,128)S(1)}, f32[32,4096]{1,0:T(8,128)}, u32[]{:S(2)}) copy-start(f32[32,4096]{1,0:T(8,128)} %get-tuple-element.84) | copy-start | bytes 1572868
  686.5 169.6 %all-to-all-start.1 = ((bf16[8,2,32768]{2,1,0:T(2,128)(2,1)}), bf16[8,2,32768]{2,1,0:T(2,128)(2,1)S(1)}, u32[]{:S(2)}, u32[]{:S(2)}) async-start(bf16[8,2,32768]{2,1,0:T(2,128)(2,1)} %reshape.83), calls=%async_computation.1 | async-start | bytes 2097152 | tf_op jit(solution)/shard_map/all_to_all | solution.py:112
  857.1 1.2 copy-start.13
Sparse Core Ops, SparseCore 0:
  11.6 621.4 all-reduce.3
where the time goes:
time: 870 us
  waiting for transfers between devices  622 us (71%)
  blocking collectives  186 us (21%)
  other arithmetic  17.4 us (2%)
  between operations  16.9 us (2%)
  matrix products  10 us (1%)
  local copies, waits for them, and re-layouts  9.87 us (1%)
    psum x1, waiting for transfers between devices, on_device(): lax.psum((local_grad, emb_grad[0].astype(jnp.float32), norm_grad[0].astyp...  622 us
    psum x1, blocking collectives, on_device(): lax.psum((local_grad, emb_grad[0].astype(jnp.float32), norm_grad[0].astyp...  159 us
    all_to_all x1, blocking collectives, on_device(): lax.all_to_all(outgoing, 'shard', split_axis=0, concat_axis=2, tiled=True)  27 us
  transfers between devices with their start and end apart: 2, of which 1 were waited for; matrix products, arithmetic and copies ran while one was open for 0% of the time, Pallas kernels for 0%

commit v1 on v0

v1 whole, which is shorter than its diff:
```python
import math

import jax
import jax.numpy as jnp
from jax import lax
from jax.sharding import Mesh, PartitionSpec as P

D = 4096
HEAD = 128
MATS = 6
NS_ITERS = 5


momentum_decay = 0.95
muon_rate = 0.02
weight_decay = 0.1
adam_rate = 0.01
beta_first = 0.9
beta_second = 0.95
adam_epsilon = 1e-08
bias_first = 1.0 - 0.9**10
bias_second = 1.0 - 0.95**10
norm_epsilon = 1e-07
quintic_a = 3.4445
quintic_b = -4.775
quintic_c = 2.0315


COLUMNS = ("x", "z_lo")
SHARD = ("z_hi", "core")
SPARE = 8


def exchange(stacked, axes):
    return lax.all_to_all(stacked, axes, split_axis=0, concat_axis=0, tiled=True)


def spread(piece, axes):
    return exchange(jnp.broadcast_to(piece[None], (lax.axis_size(axes),) + piece.shape), axes)


def split_wide(wide):
    high = lax.reduce_precision(wide, 8, 7)
    low = lax.reduce_precision(wide - high, 8, 7)
    return high.astype(jnp.bfloat16), low.astype(jnp.bfloat16)


def orthogonalize(matrix):
    widened = matrix.astype(jnp.float32)
    iterate = (widened / (jnp.sqrt(jnp.sum(widened * widened)) + norm_epsilon)).astype(jnp.bfloat16)
    for sweep in range(NS_ITERS):
        gram = jnp.dot(iterate, iterate.T, preferred_element_type=jnp.float32).astype(jnp.bfloat16)
        squared = jnp.dot(gram, gram, preferred_element_type=jnp.float32)
        blend = (quintic_b * gram.astype(jnp.float32) + quintic_c * squared).astype(jnp.bfloat16)
        iterate = (
            quintic_a * iterate.astype(jnp.float32)
            + jnp.dot(blend, iterate, preferred_element_type=jnp.float32)
        ).astype(jnp.bfloat16)
    return iterate


def slot_energy(ortho, pushed):
    return jnp.sum(ortho.astype(jnp.float32) * pushed.astype(jnp.float32)) / (
        HEAD * math.sqrt(D)
    )


def owner_slots(owners, capacity):
    order = jnp.arange(owners.shape[0], dtype=jnp.int32)
    same = (owners[:, None] == owners[None, :]) & (order[None, :] < order[:, None])
    position = jnp.sum(same.astype(jnp.int32), axis=1)
    return owners * capacity + position


def adamw(weight, grad_sum, first, second):
    first_new = beta_first * first + (1.0 - beta_first) * grad_sum
    second_new = beta_second * second + (1.0 - beta_second) * grad_sum * grad_sum
    wide_weight = weight.astype(jnp.float32)
    stepped = (
        first_new / bias_first / (jnp.sqrt(second_new / bias_second) + adam_epsilon)
        + weight_decay * wide_weight
    )
    return ((wide_weight - adam_rate * stepped).astype(jnp.bfloat16), first_new, second_new)


def on_device(
    owners,
    mat_weight,
    mat_grad,
    head_block_momentum,
    emb_weight,
    emb_grad,
    emb_first,
    emb_second,
    norm_weight,
    norm_grad,
    norm_first,
    norm_second,
    qk_weight,
    qk_grad,
    qk_first,
    qk_second,
):
    muon_scale = 0.2 * math.sqrt(max(HEAD, D))
    mats, rows, width = mat_weight.shape
    blocks = lax.axis_size("y")
    pieces = lax.axis_size(COLUMNS)
    cols = width // pieces
    block = lax.axis_index("y")
    piece = lax.axis_index(COLUMNS)
    shard = lax.axis_index(SHARD)

    grads = jnp.concatenate(
        [mat_grad[0], emb_grad[0].reshape(blocks - mats, rows, width)], axis=0
    )
    grads = grads.reshape(blocks * rows, pieces, cols).transpose(1, 0, 2)
    gains = jnp.concatenate([norm_grad[0].reshape(-1), qk_grad[0].reshape(-1)])
    gains = jnp.pad(gains, (0, SPARE * cols - gains.shape[0])).reshape(1, SPARE, cols)
    outgoing = jnp.concatenate(
        [grads, jnp.broadcast_to(gains, (pieces, SPARE, cols))], axis=1
    )
    partial = jnp.sum(exchange(outgoing, COLUMNS).astype(jnp.float32), axis=0)

    gains_high, gains_low = split_wide(partial[blocks * rows : blocks * rows + SPARE // 2])
    gains = jnp.concatenate([gains_high, gains_low], axis=0)
    outgoing = jnp.concatenate(
        [
            partial[: blocks * rows].astype(jnp.bfloat16).reshape(blocks, rows, cols),
            jnp.broadcast_to(gains[None], (blocks, SPARE, cols)),
        ],
        axis=1,
    )
    total = jnp.sum(exchange(outgoing, "y").astype(jnp.float32), axis=0)
    grad_total = total[:rows]
    gains = total[rows : rows + SPARE // 2] + total[rows + SPARE // 2 :]
    gains = gains.reshape(-1)
    norm_total = gains[: norm_weight.size].reshape(norm_weight.shape)
    qk_total = gains[norm_weight.size : norm_weight.size + qk_weight.size]
    qk_total = qk_total.reshape(qk_weight.shape)

    momentum = lax.dynamic_slice(
        head_block_momentum, (jnp.minimum(block, mats - 1), 0, piece * cols), (1, rows, cols)
    )[0]
    moment_wide = momentum_decay * momentum.astype(jnp.float32) + grad_total
    pushed = (grad_total + momentum_decay * moment_wide).astype(jnp.bfloat16)

    pushed = spread(pushed, SHARD).reshape(HEAD, cols)
    pushed = spread(pushed, COLUMNS).transpose(1, 0, 2).reshape(HEAD, width)
    ortho = orthogonalize(pushed)
    energy = slot_energy(ortho, pushed)
    own = lax.dynamic_slice(ortho, (shard * rows, piece * cols), (rows, cols))

    is_mat = block < mats
    energy_high, energy_low = split_wide(energy)
    spare = jnp.arange(SPARE, dtype=jnp.int32)[:, None]
    energies = jnp.broadcast_to(jnp.where(spare == 0, energy_high, energy_low), (SPARE, cols))
    finished = jnp.concatenate(
        [
            jnp.where(is_mat, own, grad_total.astype(jnp.bfloat16)),
            moment_wide.astype(jnp.bfloat16),
            energies,
        ],
        axis=0,
    )
    finished = spread(finished, "y")
    energies = finished[:mats, 2 * rows : 2 * rows + 2, 0].astype(jnp.float32)
    energies = energies[:, 0] + energies[:, 1]
    slots = owner_slots(owners, -(-mats // lax.axis_size(SHARD)))
    owner_sums = jnp.sum(jnp.where(slots == shard, energies, 0.0)).reshape(1, 1)
    finished = jnp.concatenate(
        [finished[:, :rows], finished[:mats, rows : 2 * rows]], axis=0
    )
    finished = spread(finished, COLUMNS).transpose(1, 2, 0, 3)
    finished = finished.reshape(blocks + mats, rows, width)
    new_weight = (
        mat_weight.astype(jnp.float32) * (1.0 - muon_rate * weight_decay)
        - muon_rate * muon_scale * finished[:mats].astype(jnp.float32)
    ).astype(jnp.bfloat16)
    new_moment = finished[blocks:]
    emb_total = finished[mats:blocks].reshape(emb_weight.shape).astype(jnp.float32)
    emb_new, emb_first_new, emb_second_new = adamw(emb_weight, emb_total, emb_first, emb_second)
    norm_new, norm_first_new, norm_second_new = adamw(
        norm_weight, norm_total, norm_first, norm_second
    )
    qk_new, qk_first_new, qk_second_new = adamw(qk_weight, qk_total, qk_first, qk_second)
    return (
        new_weight,
        new_moment,
        owner_sums,
        emb_new,
        emb_first_new,
        emb_second_new,
        norm_new,
        norm_first_new,
        norm_second_new,
        qk_new,
        qk_first_new,
        qk_second_new,
    )


def solution(mesh):
    mesh = Mesh(mesh.devices.reshape(4, 2, 8, 4, 2), ("x", "z_lo", "y", "z_hi", "core"))
    group = ("x", "z_lo", "y")
    placed = (
        P(),
        P(None, SHARD, None),
        P(group, None, SHARD, None),
        P(None, SHARD, None),
        P(SHARD, None),
        P(group, SHARD, None),
        P(SHARD, None),
        P(SHARD, None),
        P(None, SHARD),
        P(group, None, SHARD),
        P(None, SHARD),
        P(None, SHARD),
        P(),
        P(group, None, None),
        P(),
        P(),
    )
    return jax.shard_map(
        on_device,
        mesh=mesh,
        in_specs=placed,
        out_specs=(
            P(None, SHARD, None),
            P(None, SHARD, None),
            P(SHARD, None),
            P(SHARD, None),
            P(SHARD, None),
            P(SHARD, None),
            P(None, SHARD),
            P(None, SHARD),
            P(None, SHARD),
            P(),
            P(),
            P(),
        ),
        check_vma=False,
    )
```

time: 870 us -> 154 us (0.18)
  the two profiles are of different devices: /device:TPU:128 before, /device:TPU:8 now
where the time goes in v1:
time: 154 us; the launch traced here: 153 us
  blocking collectives  55.6 us (36%)
  waiting for transfers between devices  45.2 us (29%)
  starting transfers between devices  15.2 us (10%)
  other arithmetic  12.6 us (8%)
  local copies, waits for them, and re-layouts  11 us (7%)
  matrix products  8.95 us (6%)
  between operations  4.65 us (3%)
    all_to_all x3, blocking collectives, exchange(): lax.all_to_all(stacked, axes, split_axis=0, concat_axis=0, tiled=True)  55.6 us
    all_to_all x3, waiting for transfers between devices, exchange(): lax.all_to_all(stacked, axes, split_axis=0, concat_axis=0, tiled=True)  45.2 us
    all_to_all x3, starting transfers between devices, exchange(): lax.all_to_all(stacked, axes, split_axis=0, concat_axis=0, tiled=True)  15.2 us
    dot_general x5, matrix products, orthogonalize(): jnp.dot(blend, iterate, preferred_element_type=jnp.float32)  6.73 us
    convert_element_type x2, local copies, waits for them, and re-layouts, orthogonalize(): widened = matrix.astype(jnp.float32)  3.78 us
  transfers between devices with their start and end apart: 3, of which 3 were waited for; matrix products, arithmetic and copies ran while one was open for 1% of the time, Pallas kernels for 0%

profile of v1, /device:TPU:8, one launch (start us, length us, event | category | flops | bytes accessed | tf_op | source)
XLA Modules:
  0.0 153.2 jit_solution(15726893444608138291)
XLA Ops:
  0.6 0.7 copy.67
  1.3 0.7 fusion.50
  2.0 1.3 pad_maximum_fusion.1
  4.2 22.5 %all_to_all.30 = bf16[8,136,512]{2,1,0:T(8,128)(2,1)S(1)} all-to-all(bf16[8,136,512]{2,1,0:T(8,128)(2,1)S(1)} %copy.55), channel_id=1, replica_groups=mesh['x'=4,'z_lo'=2,'y'=8,'z_hi'=4,'core'=2] {'x','z_lo'}, dimensions={0} | all-to-all | bytes 2228224 | tf_op jit(solution)/shard_map/all_to_all | solution.py:35
  26.9 0.7 pad_maximum_fusion.3
  27.6 7.5 %all-to-all-start.1 = ((bf16[8,24,512]{2,1,0:T(8,128)(2,1)}), bf16[8,24,512]{2,1,0:T(8,128)(2,1)S(1)}, u32[]{:S(2)}, u32[]{:S(2)}) async-start(bf16[8,24,512]{2,1,0:T(8,128)(2,1)} %pad_maximum_fusion.3), calls=%async_computation.1 | async-start | bytes 393216 | tf_op jit(solution)/shard_map/all_to_all | solution.py:35
  35.2 8.3 %all-to-all-done.1 = bf16[8,24,512]{2,1,0:T(8,128)(2,1)S(1)} async-done(((bf16[8,24,512]{2,1,0:T(8,128)(2,1)}), bf16[8,24,512]{2,1,0:T(8,128)(2,1)S(1)}, u32[]{:S(2)}, u32[]{:S(2)}) %all-to-all-start.1) | async-done | bytes 196640 | tf_op jit(solution)/shard_map/all_to_all | solution.py:35
  43.5 0.7 add_convert_fusion
  44.2 18.2 %all_to_all.31 = bf16[8,16,512]{2,1,0:T(8,128)(2,1)S(1)} all-to-all(bf16[8,16,512]{2,1,0:T(8,128)(2,1)S(1)} %broadcast_in_dim.33), channel_id=1, replica_groups=mesh['x'=4,'z_lo'=2,'y'=8,'z_hi'=4,'core'=2] {'z_hi','core'}, dimensions={0} | all-to-all | bytes 262144 | tf_op jit(solution)/shard_map/all_to_all | solution.py:35
  62.5 1.1 broadcast_in_dim.35
  63.5 3.6 %all-to-all-start.3 = ((bf16[8,128,512]{2,1,0:T(8,128)(2,1)}), bf16[8,128,512]{2,1,0:T(8,128)(2,1)S(1)}, u32[]{:S(2)}, u32[]{:S(2)}) async-start(bf16[8,128,512]{2,1,0:T(8,128)(2,1)} %broadcast_in_dim.35), calls=%async_computation.3 | async-start | bytes 2097152 | tf_op jit(solution)/shard_map/all_to_all | solution.py:35
  67.1 15.7 %all-to-all-done.3 = bf16[8,128,512]{2,1,0:T(8,128)(2,1)S(1)} async-done(((bf16[8,128,512]{2,1,0:T(8,128)(2,1)}), bf16[8,128,512]{2,1,0:T(8,128)(2,1)S(1)}, u32[]{:S(2)}, u32[]{:S(2)}) %all-to-all-start.3) | async-done | bytes 1048608 | tf_op jit(solution)/shard_map/all_to_all | solution.py:35
  82.8 1.1 fusion.5
  84.6 1.6 %convert_bitcast_fusion = f32[128,8,512]{2,0,1:T(8,128)} fusion(bf16[8,128,512]{2,1,0:T(8,128)(2,1)S(1)} %all-to-all-done.3), kind=kLoop, calls=%fused_computation.12 | loop fusion | flops 524288 | bytes 3145728 | tf_op jit(solution)/shard_map/convert_element_type | solution.py:49
  86.3 1.9 %copy.56 = f32[128,8,512]{0,2,1:T(8,128)S(1)} copy(f32[128,8,512]{2,0,1:T(8,128)} %convert_bitcast_fusion) | data formatting | bytes 4194304 | tf_op jit(solution)/shard_map/convert_element_type | solution.py:49
  88.2 1.9 %copy.57 = f32[128,4096]{1,0:T(8,128)} copy(f32[128,4096]{0,1:T(8,128)S(1)} %bitcast.66) | data formatting | bytes 4194304 | tf_op jit(solution)/shard_map/convert_element_type | solution.py:49
  90.5 2.8 %fusion = bf16[128,4096]{1,0:T(8,128)(2,1)S(1)} fusion(bf16[128,128]{1,0:T(8,128)(2,1)S(1)} %fusion.12, f32[128,4096]{1,0:T(8,128)} %copy.57, f32[]{:T(128)S(6)} %add.119), kind=kOutput, calls=%fused_computation.5 | convolution fusion | flops 142688256 | bytes 3178500 | tf_op jit(solution)/shard_map/dot_general | solution.py:57
  95.8 0.6 fusion.3
  96.8 1.1 copy-done
  98.0 2.2 %multiply_reduce_fusion = (f32[]{:T(128)}, bf16[128,4096]{1,0:T(8,128)(2,1)}) fusion(f32[128,4096]{1,0:T(8,128)S(1)} %copy-done, bf16[128,4096]{1,0:T(8,128)(2,1)S(1)} %fusion.3, bf16[128,128]{1,0:T(8,128)(2,1)S(1)} %convolution_convert_fusion), kind=kOutput, calls=%fused_computation.16 | convolution fusion | flops 142163968 | bytes 4227076 | tf_op jit(solution)/shard_map/dot_general | solution.py:57
  103.2 0.6 compare_select_fusion.1
  103.9 0.7 fusion.45
  104.7 14.9 %all_to_all.32 = bf16[8,40,512]{2,1,0:T(8,128)(2,1)S(1)} all-to-all(bf16[8,40,512]{2,1,0:T(8,128)(2,1)S(1)} %broadcast_in_dim.69), channel_id=1, replica_groups=mesh['x'=4,'z_lo'=2,'y'=8,'z_hi'=4,'core'=2] {'y'}, dimensions={0} | all-to-all | bytes 655360 | tf_op jit(solution)/shard_map/all_to_all | solution.py:35
  119.7 1.5 broadcast_in_dim.70
  121.2 4.1 %all-to-all-start.5 = ((bf16[8,14,16,512]{3,2,1,0:T(8,128)(2,1)}), bf16[8,14,16,512]{3,2,1,0:T(8,128)(2,1)S(1)}, u32[]{:S(2)}, u32[]{:S(2)}) async-start(bf16[8,14,16,512]{3,2,1,0:T(8,128)(2,1)} %broadcast_in_dim.70), calls=%async_computation.5 | async-start | bytes 3670016 | tf_op jit(solution)/shard_map/all_to_all | solution.py:35
  125.5 0.6 fusion.59
  126.1 0.6 fusion.55
  126.9 0.6 fusion.60
  127.5 21.2 %all-to-all-done.5 = bf16[8,14,16,512]{3,2,1,0:T(8,128)(2,1)S(1)} async-done(((bf16[8,14,16,512]{3,2,1,0:T(8,128)(2,1)}), bf16[8,14,16,512]{3,2,1,0:T(8,128)(2,1)S(1)}, u32[]{:S(2)}, u32[]{:S(2)}) %all-to-all-start.5) | async-done | bytes 1835040 | tf_op jit(solution)/shard_map/all_to_all | solution.py:35
  149.9 1.0 copy.65
  150.8 1.1 subtract_convert_fusion
  151.9 1.3 fusion.22
  (60 shorter events, 6.1 us)
Async XLA Ops:
  27.6 15.8 %all-to-all-start.1 = ((bf16[8,24,512]{2,1,0:T(8,128)(2,1)}), bf16[8,24,512]{2,1,0:T(8,128)(2,1)S(1)}, u32[]{:S(2)}, u32[]{:S(2)}) async-start(bf16[8,24,512]{2,1,0:T(8,128)(2,1)} %pad_maximum_fusion.3), calls=%async_computation.1 | async-start | bytes 393216 | tf_op jit(solution)/shard_map/all_to_all | solution.py:35
  63.5 19.3 %all-to-all-start.3 = ((bf16[8,128,512]{2,1,0:T(8,128)(2,1)}), bf16[8,128,512]{2,1,0:T(8,128)(2,1)S(1)}, u32[]{:S(2)}, u32[]{:S(2)}) async-start(bf16[8,128,512]{2,1,0:T(8,128)(2,1)} %broadcast_in_dim.35), calls=%async_computation.3 | async-start | bytes 2097152 | tf_op jit(solution)/shard_map/all_to_all | solution.py:35
  96.4 1.6 %copy-start = (f32[128,4096]{1,0:T(8,128)S(1)}, f32[128,4096]{1,0:T(8,128)}, u32[]{:S(2)}) copy-start(f32[128,4096]{1,0:T(8,128)} %copy.57) | copy-start | bytes 6291460
  121.2 4.2 %copy-start.11 = (s32[6]{0:T(128)S(1)}, s32[6]{0:T(128)}, u32[]{:S(2)}) copy-start(s32[6]{0:T(128)} %param.16) | copy-start | bytes 76
  121.2 4.4 %copy-start.8 = (f32[2,128]{1,0:T(2,128)S(1)}, f32[2,128]{1,0:T(2,128)}, u32[]{:S(2)}) copy-start(f32[2,128]{1,0:T(2,128)} %param.30) | copy-start | bytes 3076
  121.2 4.4 %copy-start.9 = (f32[2,128]{1,0:T(2,128)S(1)}, f32[2,128]{1,0:T(2,128)}, u32[]{:S(2)}) copy-start(f32[2,128]{1,0:T(2,128)} %param.31) | copy-start | bytes 3076
  121.2 4.4 %copy-start.10 = (bf16[2,128]{1,0:T(2,128)(2,1)S(1)}, bf16[2,128]{1,0:T(2,128)(2,1)}, u32[]{:S(2)}) copy-start(bf16[2,128]{1,0:T(2,128)(2,1)} %param.28) | copy-start | bytes 1540
  121.2 5.0 %copy-start.5 = (f32[2,512]{1,0:T(2,128)S(1)}, f32[2,512]{1,0:T(2,128)}, u32[]{:S(2)}) copy-start(f32[2,512]{1,0:T(2,128)} %param.26) | copy-start | bytes 12292
  121.2 4.9 %copy-start.6 = (f32[2,512]{1,0:T(2,128)S(1)}, f32[2,512]{1,0:T(2,128)}, u32[]{:S(2)}) copy-start(f32[2,512]{1,0:T(2,128)} %param.27) | copy-start | bytes 12292
  121.2 4.9 %copy-start.7 = (bf16[2,512]{1,0:T(2,128)(2,1)S(1)}, bf16[2,512]{1,0:T(2,128)(2,1)}, u32[]{:S(2)}) copy-start(bf16[2,512]{1,0:T(2,128)(2,1)} %param.24) | copy-start | bytes 6148
  121.2 27.5 %all-to-all-start.5 = ((bf16[8,14,16,512]{3,2,1,0:T(8,128)(2,1)}), bf16[8,14,16,512]{3,2,1,0:T(8,128)(2,1)S(1)}, u32[]{:S(2)}, u32[]{:S(2)}) async-start(bf16[8,14,16,512]{3,2,1,0:T(8,128)(2,1)} %broadcast_in_dim.70), calls=%async_computation.5 | async-start | bytes 3670016 | tf_op jit(solution)/shard_map/all_to_all | solution.py:35
  149.7 1.2 copy-start.1
  149.8 2.1 %copy-start.2 = (f32[32,4096]{1,0:T(8,128)S(1)}, f32[32,4096]{1,0:T(8,128)}, u32[]{:S(2)}) copy-start(f32[32,4096]{1,0:T(8,128)} %param.22) | copy-start | bytes 1572868
  149.9 2.1 %copy-start.3 = (f32[32,4096]{1,0:T(8,128)S(1)}, f32[32,4096]{1,0:T(8,128)}, u32[]{:S(2)}) copy-start(f32[32,4096]{1,0:T(8,128)} %param.23) | copy-start | bytes 1572868
  149.9 2.1 %copy-start.4 = (bf16[32,4096]{1,0:T(8,128)(2,1)S(1)}, bf16[32,4096]{1,0:T(8,128)(2,1)}, u32[]{:S(2)}) copy-start(bf16[32,4096]{1,0:T(8,128)(2,1)} %param.20) | copy-start | bytes 786436

commit v2 on v1

--- a/solution.py
+++ b/solution.py
@@ -3,6 +3,8 @@
 import jax
 import jax.numpy as jnp
 from jax import lax
+from jax.experimental import pallas as pl
+from jax.experimental.pallas import tpu as pltpu
 from jax.sharding import Mesh, PartitionSpec as P
 
 D = 4096
@@ -45,24 +47,120 @@
     return high.astype(jnp.bfloat16), low.astype(jnp.bfloat16)
 
 
-def orthogonalize(matrix):
-    widened = matrix.astype(jnp.float32)
-    iterate = (widened / (jnp.sqrt(jnp.sum(widened * widened)) + norm_epsilon)).astype(jnp.bfloat16)
-    for sweep in range(NS_ITERS):
-        gram = jnp.dot(iterate, iterate.T, preferred_element_type=jnp.float32).astype(jnp.bfloat16)
-        squared = jnp.dot(gram, gram, preferred_element_type=jnp.float32)
-        blend = (quintic_b * gram.astype(jnp.float32) + quintic_c * squared).astype(jnp.bfloat16)
-        iterate = (
-            quintic_a * iterate.astype(jnp.float32)
-            + jnp.dot(blend, iterate, preferred_element_type=jnp.float32)
-        ).astype(jnp.bfloat16)
-    return iterate
-
-
-def slot_energy(ortho, pushed):
-    return jnp.sum(ortho.astype(jnp.float32) * pushed.astype(jnp.float32)) / (
-        HEAD * math.sqrt(D)
-    )
+def pack(mat_grad, emb_grad, norm_grad, qk_grad, pieces):
+    mats, rows, width = mat_grad.shape
+    embs = emb_grad.shape[0]
+    cols = width // pieces
+    taken = mats * rows + embs
+
+    def kernel(mat_ref, emb_ref, norm_ref, qk_ref, out_ref, gains_ref):
+        heads = qk_ref.shape[1]
+        gains_ref[...] = jnp.zeros_like(gains_ref)
+        gains_ref[0:2, :] = norm_ref[...].astype(jnp.float32)
+        gains_ref[2:3, 0:heads] = qk_ref[0:1, :].astype(jnp.float32)
+        gains_ref[2:3, heads : 2 * heads] = qk_ref[1:2, :].astype(jnp.float32)
+        gains = gains_ref[...].astype(jnp.bfloat16)
+        for piece in range(pieces):
+            span = slice(piece * cols, (piece + 1) * cols)
+            for mat in range(mats):
+                out_ref[piece, mat * rows : (mat + 1) * rows, :] = mat_ref[mat, :, span]
+            out_ref[piece, mats * rows : taken, :] = emb_ref[:, span]
+            out_ref[piece, taken : taken + SPARE, :] = gains
+
+    return pl.pallas_call(
+        kernel,
+        out_shape=jax.ShapeDtypeStruct((pieces, taken + SPARE, cols), jnp.bfloat16),
+        scratch_shapes=[pltpu.VMEM((SPARE, cols), jnp.float32)],
+        compiler_params=pltpu.CompilerParams(vmem_limit_bytes=8 << 20),
+        name="pack",
+    )(mat_grad, emb_grad, norm_grad, qk_grad)
+
+
+def orthogonalize(pushed, held, where, copies):
+    pieces, _, cols = pushed.shape
+    rows = held.shape[0]
+    spans = [slice(piece * cols, (piece + 1) * cols) for piece in range(pieces)]
+
+    def folded(wide):
+        return jnp.sum(wide.reshape(HEAD // 8, 8, cols), axis=0)
+
+    def kernel(where_ref, pushed_ref, held_ref, out_ref, iterate_ref, ortho_ref):
+        squares = jnp.zeros((8, cols), jnp.float32)
+        for piece in range(pieces):
+            wide = pushed_ref[piece].astype(jnp.float32)
+            squares = squares + folded(wide * wide)
+        squares = jnp.sum(jnp.sum(squares, axis=0, keepdims=True), axis=1, keepdims=True)
+        inverse = 1.0 / (jnp.sqrt(squares) + norm_epsilon)
+        for piece in range(pieces):
+            wide = pushed_ref[piece].astype(jnp.float32)
+            iterate_ref[:, spans[piece]] = (wide * inverse).astype(jnp.bfloat16)
+        energy = jnp.zeros((8, cols), jnp.float32)
+        for sweep in range(NS_ITERS):
+            iterate = iterate_ref[...]
+            gram = lax.dot_general(
+                iterate, iterate, (((1,), (1,)), ((), ())), preferred_element_type=jnp.float32
+            ).astype(jnp.bfloat16)
+            squared = jnp.dot(gram, gram, preferred_element_type=jnp.float32)
+            blend = (quintic_b * gram.astype(jnp.float32) + quintic_c * squared).astype(
+                jnp.bfloat16
+            )
+            for piece in range(pieces):
+                old = iterate_ref[:, spans[piece]]
+                new = (
+                    quintic_a * old.astype(jnp.float32)
+                    + jnp.dot(blend, old, preferred_element_type=jnp.float32)
+                ).astype(jnp.bfloat16)
+                if sweep < NS_ITERS - 1:
+                    iterate_ref[:, spans[piece]] = new
+                else:
+                    ortho_ref[piece] = new
+                    energy = energy + folded(
+                        new.astype(jnp.float32) * pushed_ref[piece].astype(jnp.float32)
+                    )
+        energy = jnp.sum(jnp.sum(energy, axis=0, keepdims=True), axis=1, keepdims=True)
+        energy = energy / (HEAD * math.sqrt(D))
+        high = energy.astype(jnp.bfloat16).astype(jnp.float32)
+        low = energy - high
+        row = lax.broadcasted_iota(jnp.int32, (SPARE, cols), 0)
+        energies = jnp.where(row == 0, high, low).astype(jnp.bfloat16)
+        start = pl.multiple_of(where_ref[1] * rows, rows)
+        own = ortho_ref[where_ref[0], pl.ds(start, rows), :]
+        for copy in range(copies):
+            out_ref[copy, 0:rows, :] = own
+            out_ref[copy, rows : 2 * rows, :] = held_ref[...]
+            out_ref[copy, 2 * rows : 2 * rows + SPARE, :] = energies
+
+    return pl.pallas_call(
+        kernel,
+        out_shape=jax.ShapeDtypeStruct((copies, 2 * rows + SPARE, cols), jnp.bfloat16),
+        in_specs=[
+            pl.BlockSpec(memory_space=pltpu.SMEM),
+            pl.BlockSpec(memory_space=pltpu.VMEM),
+            pl.BlockSpec(memory_space=pltpu.VMEM),
+        ],
+        scratch_shapes=[
+            pltpu.VMEM((HEAD, pieces * cols), jnp.bfloat16),
+            pltpu.VMEM((pieces, HEAD, cols), jnp.bfloat16),
+        ],
+        compiler_params=pltpu.CompilerParams(vmem_limit_bytes=12 << 20),
+        name="newton_schulz",
+    )(where, pushed, held)
+
+
+def fan_out(finished, mats, rows, copies):
+    blocks, _, cols = finished.shape
+
+    def kernel(finished_ref, out_ref):
+        for copy in range(copies):
+            out_ref[copy, 0:mats] = finished_ref[0:mats, 0:rows, :]
+            out_ref[copy, mats : mats + blocks] = finished_ref[:, rows : 2 * rows, :]
+
+    return pl.pallas_call(
+        kernel,
+        out_shape=jax.ShapeDtypeStruct((copies, mats + blocks, rows, cols), jnp.bfloat16),
+        compiler_params=pltpu.CompilerParams(vmem_limit_bytes=8 << 20),
+        name="fan_out",
+    )(finished)
 
 
 def owner_slots(owners, capacity):
@@ -110,15 +208,15 @@
     piece = lax.axis_index(COLUMNS)
     shard = lax.axis_index(SHARD)
 
-    grads = jnp.concatenate(
-        [mat_grad[0], emb_grad[0].reshape(blocks - mats, rows, width)], axis=0
-    )
-    grads = grads.reshape(blocks * rows, pieces, cols).transpose(1, 0, 2)
-    gains = jnp.concatenate([norm_grad[0].reshape(-1), qk_grad[0].reshape(-1)])
-    gains = jnp.pad(gains, (0, SPARE * cols - gains.shape[0])).reshape(1, SPARE, cols)
-    outgoing = jnp.concatenate(
-        [grads, jnp.broadcast_to(gains, (pieces, SPARE, cols))], axis=1
-    )
+    where = jnp.stack([piece, shard]).astype(jnp.int32)
+    momentum = lax.dynamic_slice(
+        head_block_momentum, (jnp.minimum(block, mats - 1), 0, piece * cols), (1, rows, cols)
+    )[0]
+    mat_grad, where, momentum, is_mat = lax.optimization_barrier(
+        (mat_grad, where, momentum, block < mats)
+    )
+
+    outgoing = pack(mat_grad[0], emb_grad[0], norm_grad[0], qk_grad[0], pieces)
     partial = jnp.sum(exchange(outgoing, COLUMNS).astype(jnp.float32), axis=0)
 
     gains_high, gains_low = split_wide(partial[blocks * rows : blocks * rows + SPARE // 2])
@@ -138,46 +236,28 @@
     qk_total = gains[norm_weight.size : norm_weight.size + qk_weight.size]
     qk_total = qk_total.reshape(qk_weight.shape)
 
-    momentum = lax.dynamic_slice(
-        head_block_momentum, (jnp.minimum(block, mats - 1), 0, piece * cols), (1, rows, cols)
-    )[0]
     moment_wide = momentum_decay * momentum.astype(jnp.float32) + grad_total
     pushed = (grad_total + momentum_decay * moment_wide).astype(jnp.bfloat16)
 
+    held = jnp.where(is_mat, moment_wide, grad_total).astype(jnp.bfloat16)
+
     pushed = spread(pushed, SHARD).reshape(HEAD, cols)
-    pushed = spread(pushed, COLUMNS).transpose(1, 0, 2).reshape(HEAD, width)
-    ortho = orthogonalize(pushed)
-    energy = slot_energy(ortho, pushed)
-    own = lax.dynamic_slice(ortho, (shard * rows, piece * cols), (rows, cols))
-
-    is_mat = block < mats
-    energy_high, energy_low = split_wide(energy)
-    spare = jnp.arange(SPARE, dtype=jnp.int32)[:, None]
-    energies = jnp.broadcast_to(jnp.where(spare == 0, energy_high, energy_low), (SPARE, cols))
-    finished = jnp.concatenate(
-        [
-            jnp.where(is_mat, own, grad_total.astype(jnp.bfloat16)),
-            moment_wide.astype(jnp.bfloat16),
-            energies,
-        ],
-        axis=0,
-    )
-    finished = spread(finished, "y")
+    pushed = spread(pushed, COLUMNS)
+
+    finished = exchange(orthogonalize(pushed, held, where, blocks), "y")
     energies = finished[:mats, 2 * rows : 2 * rows + 2, 0].astype(jnp.float32)
     energies = energies[:, 0] + energies[:, 1]
     slots = owner_slots(owners, -(-mats // lax.axis_size(SHARD)))
     owner_sums = jnp.sum(jnp.where(slots == shard, energies, 0.0)).reshape(1, 1)
-    finished = jnp.concatenate(
-        [finished[:, :rows], finished[:mats, rows : 2 * rows]], axis=0
-    )
-    finished = spread(finished, COLUMNS).transpose(1, 2, 0, 3)
-    finished = finished.reshape(blocks + mats, rows, width)
+    finished = exchange(fan_out(finished, mats, rows, pieces), COLUMNS)
+    finished = finished.transpose(1, 2, 0, 3).reshape(mats + blocks, rows, width)
+    ortho = finished[:mats]
+    new_moment = finished[mats : 2 * mats]
+    emb_total = finished[2 * mats :].reshape(emb_weight.shape).astype(jnp.float32)
     new_weight = (
         mat_weight.astype(jnp.float32) * (1.0 - muon_rate * weight_decay)
-        - muon_rate * muon_scale * finished[:mats].astype(jnp.float32)
+        - muon_rate * muon_scale * ortho.astype(jnp.float32)
     ).astype(jnp.bfloat16)
-    new_moment = finished[blocks:]
-    emb_total = finished[mats:blocks].reshape(emb_weight.shape).astype(jnp.float32)
     emb_new, emb_first_new, emb_second_new = adamw(emb_weight, emb_total, emb_first, emb_second)
     norm_new, norm_first_new, norm_second_new = adamw(
         norm_weight, norm_total, norm_first, norm_second

time: 154 us -> 133 us (0.86)
  blocking collectives: 55.6 us -> 88.9 us
  waiting for transfers between devices: 45.2 us -> 18.8 us
  starting transfers between devices: 15.2 us -> 3.74 us
  matrix products: 8.95 us -> 0 us
  Pallas kernels: 0 us -> 8.19 us
  other arithmetic: 12.6 us -> 4.95 us
  between operations: 4.65 us -> 0.88 us
  local copies, waits for them, and re-layouts: 11 us -> 7.42 us
    all_to_all x3 -> x5, blocking collectives: 55.6 us -> 88.9 us  [exchange(): lax.all_to_all(stacked, axes, split_axis=0, concat_axis=0, tiled=True)]
    all_to_all x3 -> x1, waiting for transfers between devices: 45.2 us -> 18.8 us  [exchange(): lax.all_to_all(stacked, axes, split_axis=0, concat_axis=0, tiled=True)]
    all_to_all x3 -> x1, starting transfers between devices: 15.2 us -> 3.74 us  [exchange(): lax.all_to_all(stacked, axes, split_axis=0, concat_axis=0, tiled=True)]
    dot_general x10 -> x0, matrix products: 8.95 us -> none  [the longest x5 6.73 us: orthogonalize(): jnp.dot(blend, iterate, preferred_element_type=jnp.float32)]
    pallas_call x0 -> x3, Pallas kernels: none -> 8.19 us  [the longest x1 6.74 us: orthogonalize(): pl.pallas_call(kernel, out_shape=jax.ShapeDtypeStruct((copies, 2 * rows +...]
    convert_element_type x3 -> x2, local copies, waits for them, and re-layouts: 4.09 us -> 0.41 us  [the longest x1 0.31 us: on_device(): finished[2 * mats:].reshape(emb_weight.shape).astype(jnp.float32)]
    unnamed x29 -> x34, local copies, waits for them, and re-layouts: 2.76 us -> 5.79 us
    broadcast_in_dim x4 -> x2, local copies, waits for them, and re-layouts: 2.57 us -> 0.09 us  [spread(): jnp.broadcast_to(piece[None], (lax.axis_size(axes),) + piece.shape)]
  transfers between devices with their start and end apart: 3 -> 1, of which waited for: 3 -> 1; matrix products, arithmetic and copies ran while one was open for 1% -> 2% of each run, Pallas kernels for 0% -> 0%
where the time goes in v2:
time: 133 us
  blocking collectives  88.9 us (67%)
  waiting for transfers between devices  18.8 us (14%)
  Pallas kernels  8.19 us (6%)
  local copies, waits for them, and re-layouts  7.42 us (6%)
  other arithmetic  4.95 us (4%)
  starting transfers between devices  3.74 us (3%)
    all_to_all x5, blocking collectives, exchange(): lax.all_to_all(stacked, axes, split_axis=0, concat_axis=0, tiled=True)  88.9 us
    all_to_all x1, waiting for transfers between devices, exchange(): lax.all_to_all(stacked, axes, split_axis=0, concat_axis=0, tiled=True)  18.8 us
    pallas_call x1, Pallas kernels, orthogonalize(): pl.pallas_call(kernel, out_shape=jax.ShapeDtypeStruct((copies, 2 * rows +...  6.74 us
    unnamed x34, local copies, waits for them, and re-layouts  5.79 us
    all_to_all x1, starting transfers between devices, exchange(): lax.all_to_all(stacked, axes, split_axis=0, concat_axis=0, tiled=True)  3.74 us
  transfers between devices with their start and end apart: 1, of which 1 were waited for; matrix products, arithmetic and copies ran while one was open for 2% of the time, Pallas kernels for 0%

profile of v2, /device:TPU:8, one launch (start us, length us, event | category | flops | bytes accessed | tf_op | source)
XLA Modules:
  0.0 132.9 jit_solution(16447357851077292558)
XLA Ops:
  0.7 1.0 copy-done
  1.8 1.1 copy-done.1
  2.9 0.9 copy-done.2
  3.9 0.7 copy-done.3
  4.6 0.7 copy-done.4
  5.2 0.1 pack.1
  5.3 22.5 %all_to_all.30 = bf16[8,136,512]{2,1,0:T(8,128)(2,1)S(1)} all-to-all(bf16[8,136,512]{2,1,0:T(8,128)(2,1)S(1)} %pack.1), channel_id=1, replica_groups=mesh['x'=4,'z_lo'=2,'y'=8,'z_hi'=4,'core'=2] {'x','z_lo'}, dimensions={0} | all-to-all | bytes 2228224 | tf_op jit(solution)/shard_map/all_to_all | solution.py:37
  27.8 0.2 convert_reduce_fusion
  28.1 15.6 %all_to_all.31 = bf16[8,24,512]{2,1,0:T(8,128)(2,1)S(1)} all-to-all(bf16[8,24,512]{2,1,0:T(8,128)(2,1)S(1)} %pad_maximum_fusion), channel_id=1, replica_groups=mesh['x'=4,'z_lo'=2,'y'=8,'z_hi'=4,'core'=2] {'y'}, dimensions={0} | all-to-all | bytes 393216 | tf_op jit(solution)/shard_map/all_to_all | solution.py:37
  43.7 18.2 %all_to_all.32 = bf16[8,16,512]{2,1,0:T(8,128)(2,1)S(1)} all-to-all(bf16[8,16,512]{2,1,0:T(8,128)(2,1)S(1)} %broadcast_in_dim.12), channel_id=1, replica_groups=mesh['x'=4,'z_lo'=2,'y'=8,'z_hi'=4,'core'=2] {'z_hi','core'}, dimensions={0} | all-to-all | bytes 262144 | tf_op jit(solution)/shard_map/all_to_all | solution.py:37
  62.0 0.1 broadcast_in_dim.14
  62.1 18.4 %all_to_all.33.pushed_ref = bf16[8,128,512]{2,1,0:T(8,128)(2,1)S(1)} all-to-all(bf16[8,128,512]{2,1,0:T(8,128)(2,1)S(1)} %broadcast_in_dim.14), channel_id=1, replica_groups=mesh['x'=4,'z_lo'=2,'y'=8,'z_hi'=4,'core'=2] {'x','z_lo'}, dimensions={0} | all-to-all | bytes 2097152 | tf_op jit(solution)/shard_map/all_to_all | solution.py:37
  80.4 6.7 %newton_schulz.1 = bf16[8,40,512]{2,1,0:T(8,128)(2,1)S(1)} custom-call(s32[2]{0:T(128)S(1)} %pad_add_fusion.where_ref, bf16[8,128,512]{2,1,0:T(8,128)(2,1)S(1)} %all_to_all.33.pushed_ref, bf16[16,512]{1,0:T(8,128)(2,1)S(1)} %get-tuple-element.31.held_ref), custom_call_target="tpu_custom_call" | custom-call | tf_op jit(solution)/shard_map/newton_schulz/pallas_call | solution.py:133
  87.2 14.2 %all_to_all.34.finished_ref = bf16[8,40,512]{2,1,0:T(8,128)(2,1)S(1)} all-to-all(bf16[8,40,512]{2,1,0:T(8,128)(2,1)S(1)} %newton_schulz.1), channel_id=1, replica_groups=mesh['x'=4,'z_lo'=2,'y'=8,'z_hi'=4,'core'=2] {'y'}, dimensions={0} | all-to-all | bytes 655360 | tf_op jit(solution)/shard_map/all_to_all | solution.py:37
  101.4 1.4 %fan_out.1 = bf16[8,14,16,512]{3,2,1,0:T(8,128)(2,1)} custom-call(bf16[8,40,512]{2,1,0:T(8,128)(2,1)S(1)} %all_to_all.34.finished_ref), custom_call_target="tpu_custom_call" | custom-call | tf_op jit(solution)/shard_map/fan_out/pallas_call | solution.py:158
  102.8 3.7 %all-to-all-start.5 = ((bf16[8,14,16,512]{3,2,1,0:T(8,128)(2,1)}), bf16[8,14,16,512]{3,2,1,0:T(8,128)(2,1)S(1)}, u32[]{:S(2)}, u32[]{:S(2)}) async-start(bf16[8,14,16,512]{3,2,1,0:T(8,128)(2,1)} %fan_out.1), calls=%async_computation.5 | async-start | bytes 3670016 | tf_op jit(solution)/shard_map/all_to_all | solution.py:37
  106.5 0.2 convert_reduce_fusion.2
  106.8 0.6 fusion.14
  107.4 0.6 fusion.10
  108.0 0.1 copy.39
  108.1 0.6 fusion.15
  108.7 18.8 %all-to-all-done.5 = bf16[8,14,16,512]{3,2,1,0:T(8,128)(2,1)S(1)} async-done(((bf16[8,14,16,512]{3,2,1,0:T(8,128)(2,1)}), bf16[8,14,16,512]{3,2,1,0:T(8,128)(2,1)S(1)}, u32[]{:S(2)}, u32[]{:S(2)}) %all-to-all-start.5) | async-done | bytes 1835040 | tf_op jit(solution)/shard_map/all_to_all | solution.py:37
  127.6 0.2 multiply_bitcast_fusion
  127.8 0.3 copy.40
  128.1 0.3 copy.43
  128.4 0.1 copy.41
  128.6 0.9 copy.42
  129.5 0.5 copy-done.5
  130.0 1.1 subtract_convert_fusion
  131.1 0.4 copy-done.7
  131.4 0.1 copy-done.8
  131.6 1.3 fusion.2
  (39 shorter events, 0.4 us)
Async XLA Ops:
  0.6 1.1 copy-start
  1.8 1.1 copy-start.1
  2.9 0.9 copy-start.2
  3.9 0.7 copy-start.3
  4.6 0.7 copy-start.4
  102.7 3.8 %copy-start.15 = (s32[6]{0:T(128)S(1)}, s32[6]{0:T(128)}, u32[]{:S(2)}) copy-start(s32[6]{0:T(128)} %param.16) | copy-start | bytes 76
  102.7 4.0 %copy-start.12 = (f32[2,128]{1,0:T(2,128)S(1)}, f32[2,128]{1,0:T(2,128)}, u32[]{:S(2)}) copy-start(f32[2,128]{1,0:T(2,128)} %param.30) | copy-start | bytes 3076
  102.7 4.0 %copy-start.13 = (f32[2,128]{1,0:T(2,128)S(1)}, f32[2,128]{1,0:T(2,128)}, u32[]{:S(2)}) copy-start(f32[2,128]{1,0:T(2,128)} %param.31) | copy-start | bytes 3076
  102.7 4.0 %copy-start.14 = (bf16[2,128]{1,0:T(2,128)(2,1)S(1)}, bf16[2,128]{1,0:T(2,128)(2,1)}, u32[]{:S(2)}) copy-start(bf16[2,128]{1,0:T(2,128)(2,1)} %param.28) | copy-start | bytes 1540
  102.7 4.6 %copy-start.9 = (f32[2,512]{1,0:T(2,128)S(1)}, f32[2,512]{1,0:T(2,128)}, u32[]{:S(2)}) copy-start(f32[2,512]{1,0:T(2,128)} %param.26) | copy-start | bytes 12292
  102.8 4.6 %copy-start.10 = (f32[2,512]{1,0:T(2,128)S(1)}, f32[2,512]{1,0:T(2,128)}, u32[]{:S(2)}) copy-start(f32[2,512]{1,0:T(2,128)} %param.27) | copy-start | bytes 12292
  102.8 4.6 %copy-start.11 = (bf16[2,512]{1,0:T(2,128)(2,1)S(1)}, bf16[2,512]{1,0:T(2,128)(2,1)}, u32[]{:S(2)}) copy-start(bf16[2,512]{1,0:T(2,128)(2,1)} %param.24) | copy-start | bytes 6148
  102.8 24.7 %all-to-all-start.5 = ((bf16[8,14,16,512]{3,2,1,0:T(8,128)(2,1)}), bf16[8,14,16,512]{3,2,1,0:T(8,128)(2,1)S(1)}, u32[]{:S(2)}, u32[]{:S(2)}) async-start(bf16[8,14,16,512]{3,2,1,0:T(8,128)(2,1)} %fan_out.1), calls=%async_computation.5 | async-start | bytes 3670016 | tf_op jit(solution)/shard_map/all_to_all | solution.py:37
  128.6 1.4 %copy-start.5 = (bf16[6,16,4096]{2,1,0:T(8,128)(2,1)S(1)}, bf16[6,16,4096]{2,1,0:T(8,128)(2,1)}, u32[]{:S(2)}) copy-start(bf16[6,16,4096]{2,1,0:T(8,128)(2,1)} %param.17) | copy-start | bytes 2359300
  130.0 1.1 copy-start.6
  130.0 1.4 %copy-start.7 = (f32[32,4096]{1,0:T(8,128)S(1)}, f32[32,4096]{1,0:T(8,128)}, u32[]{:S(2)}) copy-start(f32[32,4096]{1,0:T(8,128)} %param.23) | copy-start | bytes 1572868
  130.0 1.5 %copy-start.8 = (bf16[32,4096]{1,0:T(8,128)(2,1)S(1)}, bf16[32,4096]{1,0:T(8,128)(2,1)}, u32[]{:S(2)}) copy-start(bf16[32,4096]{1,0:T(8,128)(2,1)} %param.20) | copy-start | bytes 786436
